TPU v7x, 32 devices: a whole 2x2x4 slice. The times are simulated.
32 devices in a mesh: lat: 8 (over y, x, core), lev: 4 (over z).
Axes of the slice: x: 2, y: 2, z: 4, core: 2. Of those that a mesh axis runs over, the one named last changes fastest.
Arguments:
- activations: bfloat16 [176, 819200], P(None, ('lat', 'lev')), may hold values from -6 to 6
- out_cotangent: bfloat16 [176, 819200], P(None, ('lat', 'lev')), may hold values from -6 to 6
- weight_in: bfloat16 [176, 384], replicated, may hold values from -0.4375 to 0.4375
- weight_mid: bfloat16 [384, 384], replicated, may hold values from -0.3125 to 0.3125
- weight_out: bfloat16 [176, 384], replicated, may hold values from -0.3125 to 0.3125
- legendre: bfloat16 [640, 320, 640], P(('lat', 'lev')), may hold values from -0.25 to 0.25
- level_inverse: bfloat16 [88, 88, 640], replicated, may hold values from -0.625 to 0.625
- wave_order: int32 [640], replicated, may hold values from 0 to 639, each once
Outputs:
- grad_input: float32 [176, 384], replicated
- grad_middle: float32 [384, 384], replicated
- grad_output: float32 [176, 384], replicated
- grid_cotangent: float32 [176, 640, 1280], P(None, ('lat', 'lev'))
Inputs may be any that keep to these rules, and one draw needn't show every extreme that they name: wave_order is a permutation of 0 to 639; the device at index d of lat and lev taken together (lat major) holds the d-th block of slots of legendre.
All inputs are finite; a program needn't handle non-finite values.
Results may differ from a plain program's by a relative error of at most 0.017.
Values may be sent and summed in bfloat16 or wider, within the bound.
A program may use at most 320 MiB of HBM per device.

v0:
```python
import math

import jax
import jax.numpy as jnp
from jax import lax
from jax.sharding import PartitionSpec as P

BF = jnp.bfloat16
F32 = jnp.float32


def silu_slope(values):
    sigmoid = jax.nn.sigmoid(values)
    return sigmoid * (1.0 + values * (1.0 - sigmoid))


def first_dims(left, right):
    return lax.dot_general(left, right, (((0,), (0,)), ((), ())), preferred_element_type=F32)


def last_dims(left, right):
    return lax.dot_general(left, right, (((1,), (1,)), ((), ())), preferred_element_type=F32)


def wave_tables(wavenumbers, points):
    wave_count = wavenumbers.shape[0]
    columns = lax.broadcasted_iota(jnp.int32, (points, wave_count), 0)
    phase_int = columns * wavenumbers[None, :] % points
    angles = phase_int.astype(F32) * (2.0 * math.pi / points)
    return (jnp.cos(angles), jnp.sin(angles))


def full_legendre(legendre, wave_local):
    slots, half, degrees = legendre.shape
    row = lax.broadcasted_iota(jnp.int32, (2 * half, half), 0)
    col = lax.broadcasted_iota(jnp.int32, (2 * half, half), 1)
    spread = ((row == col) | (row + col == 2 * half - 1)).astype(BF)
    both = jnp.einsum("pi,sil->spl", spread, legendre, preferred_element_type=F32)
    shape = (slots, 2 * half, degrees)
    degree = lax.broadcasted_iota(jnp.int32, shape, 2)
    lat = lax.broadcasted_iota(jnp.int32, shape, 1)
    wave = wave_local[:, None, None]
    flip = (lat >= half) & ((degree + wave) % 2 == 1)
    both = jnp.where(flip, -both, both)
    return jnp.where(degree >= wave, both, 0.0).astype(BF)


def on_device(
    activations,
    out_cotangent,
    weight_in,
    weight_mid,
    weight_out,
    legendre,
    level_inverse,
    wave_order,
):
    features, columns = activations.shape
    n_lat, n_lev = lax.axis_size("lat"), lax.axis_size("lev")
    n_dev = n_lat * n_lev
    slot_count, half, degrees = legendre.shape
    nlat = 2 * half
    levels = level_inverse.shape[0]
    fields = features // levels
    lat_rows = nlat // n_lat
    lon_rows = columns // lat_rows
    nlon = lon_rows * n_lev
    waves = wave_order.shape[0]
    sub = lat_rows // n_lev
    both_axes = ("lat", "lev")

    pre_first = first_dims(weight_in, activations)
    hidden_first = jax.nn.silu(pre_first).astype(BF)
    pre_second = first_dims(weight_mid, hidden_first)
    hidden_second = jax.nn.silu(pre_second).astype(BF)
    back_second = first_dims(weight_out, out_cotangent)
    delta_second = (back_second * silu_slope(pre_second)).astype(BF)
    back_first = jnp.dot(weight_mid, delta_second, preferred_element_type=F32)
    delta_first = (back_first * silu_slope(pre_first)).astype(BF)

    cosines, sines = wave_tables(wave_order, nlon)
    root_points = math.sqrt(nlon)
    forward_table = (jnp.stack([cosines, -sines], axis=2) / root_points).astype(BF)
    forward_table = forward_table.reshape(nlon, 2 * waves)
    wave_local = lax.dynamic_slice_in_dim(
        wave_order, lax.axis_index(both_axes) * slot_count, slot_count
    )
    table = full_legendre(legendre, wave_local)
    inverse_levels = level_inverse.transpose(2, 0, 1)
    wave_weights = jnp.where(wave_order > 0, 2.0, 1.0).astype(F32) / root_points
    inverse_table = (
        jnp.stack([cosines.T, -sines.T], axis=1) * wave_weights[:, None, None]
    ).astype(BF).reshape(2 * waves, nlon)

    grid_rows = []
    for a in range(fields):
        part = jnp.dot(
            weight_in[a * levels : (a + 1) * levels], delta_first, preferred_element_type=F32
        ).astype(BF)
        part = part.reshape(levels, n_lev, sub * lon_rows).transpose(1, 0, 2)
        grid_rows.append(lax.all_to_all(part, "lev", split_axis=0, concat_axis=0, tiled=True))

    partials = (
        last_dims(activations, delta_first),
        last_dims(hidden_first, delta_second),
        last_dims(out_cotangent, hidden_second),
    )
    forward_table, partials, grid_rows[0] = lax.optimization_barrier(
        (forward_table, partials, grid_rows[0])
    )
    totals = lax.psum(partials, both_axes)
    grad_scale = 1.0 / math.sqrt(nlat * nlon)

    gathered = []
    for a in range(fields):
        if a == fields - 1:
            table, inverse_levels, inverse_table, grid_rows[a] = lax.optimization_barrier(
                (table, inverse_levels, inverse_table, grid_rows[a])
            )
        rows = grid_rows[a].reshape(n_lev, levels, sub, lon_rows)
        rows = rows.transpose(2, 1, 0, 3).reshape(sub * levels, nlon)
        fourier = lax.dot_general(
            forward_table, rows, (((0,), (1,)), ((), ())), preferred_element_type=F32
        ).astype(BF)
        fourier = fourier.reshape(waves, 2, sub * levels)
        gathered.append(
            lax.all_to_all(fourier, both_axes, split_axis=0, concat_axis=0, tiled=True)
        )

    zonal = []
    for a in range(fields):
        fourier = gathered[a].reshape(n_dev, slot_count, 2, sub, levels)
        fourier = fourier.transpose(1, 2, 4, 0, 3).reshape(slot_count, 2 * levels, nlat)
        coeffs = jnp.einsum("sfi,sil->sfl", fourier, table, preferred_element_type=F32).astype(BF)
        coeffs = coeffs.reshape(slot_count, 2, levels, degrees)
        solved = jnp.einsum(
            "srkl,lkq->srql", coeffs, inverse_levels, preferred_element_type=F32
        ).astype(BF)
        rows = jnp.einsum("srql,sil->siqr", solved, table, preferred_element_type=F32).astype(BF)
        rows = rows.reshape(slot_count, n_dev, sub, levels, 2).transpose(1, 0, 4, 2, 3)
        rows = rows.reshape(waves, 2, sub * levels)
        zonal.append(lax.all_to_all(rows, both_axes, split_axis=0, concat_axis=0, tiled=True))

    outs = []
    for a in range(fields):
        out = lax.dot_general(
            zonal[a].reshape(2 * waves, sub * levels),
            inverse_table,
            (((0,), (0,)), ((), ())),
            preferred_element_type=F32,
        )
        outs.append(out.reshape(sub, levels, nlon))
    grid_cotangent = jnp.concatenate(outs, axis=1).transpose(1, 0, 2)
    return (totals[0] * grad_scale, totals[1] * grad_scale, totals[2] * grad_scale, grid_cotangent)


def solution(mesh):
    in_specs = (
        P(None, ("lat", "lev")),
        P(None, ("lat", "lev")),
        P(),
        P(),
        P(),
        P(("lat", "lev"), None, None),
        P(),
        P(),
    )
    out_specs = (P(), P(), P(), P(None, ("lat", "lev"), None))
    return jax.shard_map(
        on_device, mesh=mesh, in_specs=in_specs, out_specs=out_specs, check_vma=False
    )
```

profile of v0, /device:TPU:0, one launch (start us, length us, event | category | flops | bytes accessed | tf_op | source)
XLA Modules:
  0.0 1027.8 jit_solution(4106347965929480)
XLA Ops:
  7.2 25.3 %multiply_convert_fusion = (bf16[384,25600]{1,0:T(8,128)(2,1)}, f32[384,25600]{1,0:T(8,128)}) fusion(bf16[176,384]{1,0:T(8,128)(2,1)} %param.10, bf16[176,25600]{1,0:T(8,128)(2,1)} %param.8), kind=kOutput, calls=%fused_computation.17 | convolution fusion | flops 3509452800 | bytes 68128768 | tf_op jit(solution)/shard_map/dot_general | solution.py:18
  32.5 23.3 %fusion.62 = f32[25600,384]{0,1:T(8,128)} fusion(bf16[384,25600]{1,0:T(8,128)(2,1)} %get-tuple-element.29, bf16[384,384]{1,0:T(8,128)(2,1)S(1)} %copy-done), kind=kOutput, calls=%fused_computation.91 | convolution fusion | flops 7549747200 | bytes 59277312 | tf_op jit(solution)/shard_map/dot_general | solution.py:18
  55.8 27.9 %fusion.7 = bf16[384,25600]{1,0:T(8,128)(2,1)} fusion(f32[25600,384]{0,1:T(8,128)} %fusion.62, bf16[176,384]{1,0:T(8,128)(2,1)S(1)} %copy-done.6, bf16[176,25600]{1,0:T(8,128)(2,1)} %param.9), kind=kOutput, calls=%fused_computation.15 | convolution fusion | flops 3548774400 | bytes 68128768 | tf_op jit(solution)/shard_map/dot_general | solution.py:18
  83.7 38.6 %fusion = bf16[384,25600]{1,0:T(8,128)(2,1)} fusion(f32[384,25600]{1,0:T(8,128)} %get-tuple-element.30, bf16[384,384]{1,0:T(8,128)(2,1)S(1)} %copy-done, bf16[384,25600]{1,0:T(8,128)(2,1)} %fusion.7), kind=kOutput, calls=%fused_computation.5 | convolution fusion | flops 7638220800 | bytes 78938112 | tf_op jit(solution)/shard_map/dot_general | solution.py:78
  122.3 10.0 convolution_convert_fusion.1
  134.7 6.8 all-to-all-start
  141.5 12.2 %convolution_convert_fusion = bf16[25600,88]{0,1:T(8,128)(2,1)} fusion(bf16[384,25600]{1,0:T(8,128)(2,1)} %fusion, bf16[176,384]{1,0:T(8,128)(2,1)S(1)} %copy-done.4), kind=kOutput, calls=%fused_computation.28 | convolution fusion | flops 1732403200 | bytes 24233984 | tf_op jit(solution)/shard_map/dot_general | solution.py:97
  153.7 13.3 %fusion.39 = (f32[1280,640,1]{1,0,2:T(8,128)S(1)}, f32[1280,640,1]{1,0,2:T(8,128)S(1)}) fusion(s32[640]{0:T(1024)S(1)} %copy-done.5), kind=kLoop, calls=%fused_computation.69 | loop fusion | flops 8192000 | bytes 6556160 | tf_op jit(solution)/shard_map/cos | solution.py:30
  167.0 15.8 %fusion.36 = (f32[640,1,1280]{2,0,1:T(8,128)}, f32[640,1,1280]{2,0,1:T(8,128)}) fusion(s32[640]{0:T(1024)S(1)} %copy-done.5), kind=kLoop, calls=%fused_computation.64 | loop fusion | flops 8192000 | bytes 6556160 | tf_op jit(solution)/shard_map/cos | solution.py:30
  185.2 10.5 %copy.95 = bf16[1280,640,2]{0,2,1:T(2,128)(2,1)} copy(bf16[1280,640,2]{1,0,2:T(8,128)(2,1)} %fusion.23) | data formatting | bytes 6553600 | tf_op jit(solution)/shard_map/convert_element_type | solution.py:83
  195.7 7.9 convert_element_type.106
  208.3 6.1 pad_maximum_fusion
  214.5 10.6 %copy.99 = f32[640,2,1280]{2,1,0:T(2,128)} copy(f32[640,2,1280]{2,0,1:T(8,128)} %pad_maximum_fusion) | data formatting | bytes 13107200 | tf_op jit(solution)/shard_map/stack | solution.py:92
  225.0 8.8 stack.14
  239.2 16.2 %convolution_bitcast_fusion = f32[176,384]{1,0:T(8,128)} fusion(bf16[384,25600]{1,0:T(8,128)(2,1)} %fusion, bf16[176,25600]{1,0:T(8,128)(2,1)} %param.8), kind=kOutput, calls=%fused_computation.77 | convolution fusion | flops 3460300800 | bytes 28942336 | tf_op jit(solution)/shard_map/dot_general | solution.py:22
  255.4 18.2 %fusion.63 = f32[384,384]{1,0:T(8,128)} fusion(bf16[384,25600]{1,0:T(8,128)(2,1)} %get-tuple-element.29, bf16[384,25600]{1,0:T(8,128)(2,1)} %fusion.7), kind=kOutput, calls=%fused_computation.92 | convolution fusion | flops 7549747200 | bytes 39911424 | tf_op jit(solution)/shard_map/dot_general | solution.py:22
  279.2 21.8 %fusion.50 = f32[176,384]{1,0:T(8,128)} fusion(bf16[176,25600]{1,0:T(8,128)(2,1)} %param.9, f32[25600,384]{0,1:T(8,128)} %fusion.62), kind=kOutput, calls=%fused_computation.76 | convolution fusion | flops 3509452800 | bytes 48603136 | tf_op jit(solution)/shard_map/dot_general | solution.py:22
  301.0 10.7 %reshape.232 = bf16[4,88,20,320]{3,2,1,0:T(8,128)(2,1)} reshape(bf16[4,88,6400]{2,1,0:T(8,128)(2,1)} %all-to-all-done) | data formatting | bytes 9011200 | tf_op jit(solution)/shard_map/reshape | solution.py:120
  311.7 9.4 copy.101
  321.1 9.8 reshape.233
  330.8 10.2 convolution_convert_fusion.3
  341.1 7.4 copy.102
  348.5 10.0 reshape.234
  358.4 20.7 %all-to-all-done.1 = bf16[4,88,6400]{2,1,0:T(8,128)(2,1)} async-done(((bf16[4,88,6400]{2,1,0:T(8,128)(2,1)}), bf16[4,88,6400]{2,1,0:T(8,128)(2,1)}, u32[]{:S(2)}, u32[]{:S(2)}) %all-to-all-start.1) | async-done | bytes 4505632 | tf_op jit(solution)/shard_map/all_to_all | solution.py:101
  383.0 19.7 %fusion.12 = bf16[20,640,640]{2,1,0:T(8,128)(2,1)} fusion(s32[20]{0:T(128)S(1)} %dynamic_slice.3, pred[640]{0:T(1024)(128)(4,1)S(1)} %iota_compare_fusion.3, bf16[20,320,640]{2,1,0:T(8,128)(2,1)} %param.13), kind=kOutput, calls=%fused_computation.22 | convolution fusion | flops 5399347200 | bytes 24576720 | tf_op jit(solution)/shard_map/pi,sil->spl/dot_general | solution.py:38
  402.7 10.7 %reshape.241 = bf16[4,88,20,320]{3,2,1,0:T(8,128)(2,1)} reshape(bf16[4,88,6400]{2,1,0:T(8,128)(2,1)} %all-to-all-done.1) | data formatting | bytes 9011200 | tf_op jit(solution)/shard_map/reshape | solution.py:120
  413.4 9.4 copy.113
  422.8 9.8 reshape.242
  432.6 10.3 convolution_convert_fusion.2
  442.9 7.2 copy.114
  450.1 10.4 %reshape.243 = bf16[640,2,1760]{2,1,0:T(2,128)(2,1)} reshape(bf16[1280,1760]{1,0:T(8,128)(2,1)} %copy.114) | data formatting | bytes 9011200 | tf_op jit(solution)/shard_map/reshape | solution.py:125
  460.4 23.0 %all-to-all-done.2 = bf16[640,2,1760]{2,1,0:T(2,128)(2,1)} async-done(((bf16[640,2,1760]{2,1,0:T(2,128)(2,1)}), bf16[640,2,1760]{2,1,0:T(2,128)(2,1)}, u32[]{:S(2)}, u32[]{:S(2)}) %all-to-all-start.2) | async-done | bytes 4505632 | tf_op jit(solution)/shard_map/all_to_all | solution.py:127
  483.5 6.0 all-to-all-start.4
  489.4 18.7 %copy.128 = bf16[640,88,88,1]{2,1,3,0:T(8,128)(2,1)} copy(bf16[640,88,88,1]{0,2,1,3:T(8,128)(2,1)} %bitcast.155) | data formatting | bytes 19824640 | tf_op jit(solution)/shard_map/optimization_barrier | solution.py:117
  513.1 13.0 %reshape.235 = bf16[32,20,2,20,88]{4,3,1,0,2:T(8,128)(2,1)} reshape(bf16[640,2,1760]{2,0,1:T(8,128)(2,1)} %copy.103) | data formatting | bytes 9011200 | tf_op jit(solution)/shard_map/reshape | solution.py:132
  526.0 11.0 %copy.104 = bf16[20,2,88,32,20]{2,1,4,3,0:T(2,128)(2,1)} copy(bf16[20,2,88,32,20]{2,4,0,3,1:T(8,128)(2,1)} %bitcast.141) | data formatting | bytes 9011200 | tf_op jit(solution)/shard_map/transpose | solution.py:133
  537.0 13.6 %reshape.236 = bf16[20,176,640]{1,2,0:T(8,128)(2,1)} reshape(bf16[20,2,88,32,20]{2,1,4,3,0:T(2,128)(2,1)} %copy.104) | data formatting | bytes 9011200 | tf_op jit(solution)/shard_map/reshape | solution.py:133
  550.6 13.9 %convolution_convert_fusion.5 = bf16[20,176,640]{2,1,0:T(8,128)(2,1)} fusion(bf16[20,176,640]{1,2,0:T(8,128)(2,1)} %reshape.236, bf16[20,640,640]{2,1,0:T(8,128)(2,1)} %fusion.12), kind=kOutput, calls=%fused_computation.73 | convolution fusion | flops 2885836800 | bytes 25395200 | tf_op jit(solution)/shard_map/sfi,sil->sfl/dot_general | solution.py:134
  564.6 10.0 copy.107
  574.6 11.6 %convert_bitcast_fusion.1 = bf16[20,2,88,640]{2,0,1,3:T(8,128)(2,1)} fusion(bf16[640,88,88,1]{2,1,3,0:T(8,128)(2,1)} %copy.128, bf16[20,2,88,640]{2,0,1,3:T(8,128)(2,1)} %copy.107), kind=kOutput, calls=%fused_computation.37 | convolution fusion | flops 398745600 | bytes 18923520 | tf_op jit(solution)/shard_map/srkl,lkq->srql/dot_general | solution.py:136
  586.2 14.9 %convert_bitcast_fusion.3 = bf16[20,640,88,2]{1,2,3,0:T(8,128)(2,1)} fusion(bf16[20,2,88,640]{2,0,1,3:T(8,128)(2,1)} %convert_bitcast_fusion.1, bf16[20,640,640]{2,1,0:T(8,128)(2,1)} %fusion.12), kind=kOutput, calls=%fused_computation.51 | convolution fusion | flops 2885836800 | bytes 25395200 | tf_op jit(solution)/shard_map/srql,sil->siqr/dot_general | solution.py:139
  601.1 14.2 %copy.109 = bf16[20,640,88,2]{2,3,1,0:T(2,128)(2,1)} copy(bf16[20,640,88,2]{1,2,3,0:T(8,128)(2,1)} %convert_bitcast_fusion.3) | data formatting | bytes 9011200 | tf_op jit(solution)/shard_map/convert_element_type | solution.py:139
  615.3 7.9 copy.134
  623.3 15.7 %reshape.255 = bf16[640,2,1760]{2,1,0:T(2,128)(2,1)} reshape(bf16[32,20,2,20,88]{4,3,2,1,0:T(8,128)(2,1)} %copy.134) | data formatting | bytes 9011200 | tf_op jit(solution)/shard_map/reshape | solution.py:141
  639.0 5.9 all-to-all-start.3
  649.8 13.0 %reshape.244 = bf16[32,20,2,20,88]{4,3,1,0,2:T(8,128)(2,1)} reshape(bf16[640,2,1760]{2,0,1:T(8,128)(2,1)} %copy.115) | data formatting | bytes 9011200 | tf_op jit(solution)/shard_map/reshape | solution.py:132
  662.8 11.0 %copy.116 = bf16[20,2,88,32,20]{2,1,4,3,0:T(2,128)(2,1)} copy(bf16[20,2,88,32,20]{2,4,0,3,1:T(8,128)(2,1)} %bitcast.142) | data formatting | bytes 9011200 | tf_op jit(solution)/shard_map/transpose | solution.py:133
  673.8 13.6 %reshape.245 = bf16[20,176,640]{1,2,0:T(8,128)(2,1)} reshape(bf16[20,2,88,32,20]{2,1,4,3,0:T(2,128)(2,1)} %copy.116) | data formatting | bytes 9011200 | tf_op jit(solution)/shard_map/reshape | solution.py:133
  687.4 13.9 %convolution_convert_fusion.4 = bf16[20,176,640]{2,1,0:T(8,128)(2,1)} fusion(bf16[20,176,640]{1,2,0:T(8,128)(2,1)} %reshape.245, bf16[20,640,640]{2,1,0:T(8,128)(2,1)} %fusion.12), kind=kOutput, calls=%fused_computation.72 | convolution fusion | flops 2885836800 | bytes 25395200 | tf_op jit(solution)/shard_map/sfi,sil->sfl/dot_general | solution.py:134
  701.3 10.0 copy.119
  711.3 11.6 %convert_bitcast_fusion = bf16[20,2,88,640]{2,0,1,3:T(8,128)(2,1)} fusion(bf16[640,88,88,1]{2,1,3,0:T(8,128)(2,1)} %copy.128, bf16[20,2,88,640]{2,0,1,3:T(8,128)(2,1)} %copy.119), kind=kOutput, calls=%fused_computation.36 | convolution fusion | flops 398745600 | bytes 18923520 | tf_op jit(solution)/shard_map/srkl,lkq->srql/dot_general | solution.py:136
  722.9 14.9 %convert_bitcast_fusion.2 = bf16[20,640,88,2]{1,2,3,0:T(8,128)(2,1)} fusion(bf16[20,2,88,640]{2,0,1,3:T(8,128)(2,1)} %convert_bitcast_fusion, bf16[20,640,640]{2,1,0:T(8,128)(2,1)} %fusion.12), kind=kOutput, calls=%fused_computation.50 | convolution fusion | flops 2885836800 | bytes 25395200 | tf_op jit(solution)/shard_map/srql,sil->siqr/dot_general | solution.py:139
  737.8 14.3 %copy.121 = bf16[20,640,88,2]{2,3,1,0:T(2,128)(2,1)} copy(bf16[20,640,88,2]{1,2,3,0:T(8,128)(2,1)} %convert_bitcast_fusion.2) | data formatting | bytes 9011200 | tf_op jit(solution)/shard_map/convert_element_type | solution.py:139
  752.1 8.1 copy.137
  760.1 15.7 %reshape.256 = bf16[640,2,1760]{2,1,0:T(2,128)(2,1)} reshape(bf16[32,20,2,20,88]{4,3,2,1,0:T(8,128)(2,1)} %copy.137) | data formatting | bytes 9011200 | tf_op jit(solution)/shard_map/reshape | solution.py:141
  775.8 5.9 all-to-all-start.5
  782.5 177.2 %all-reduce.3.cloned.1.call-done = (f32[176,384]{1,0:T(8,128)}, f32[384,384]{1,0:T(8,128)}, f32[176,384]{1,0:T(8,128)}) async-done(((f32[176,384]{1,0:T(8,128)}, f32[384,384]{1,0:T(8,128)}, f32[176,384]{1,0:T(8,128)}), (f32[176,384]{1,0:T(8,128)}, f32[384,384]{1,0:T(8,128)}, f32[176,384]{1,0:T(8,128)})) %all-reduce.3.cloned.1.call-update) | async-done | bytes 1130512 | tf_op jit(solution)/shard_map/psum | solution.py:111
  963.5 10.3 %reshape.240 = bf16[1280,1760]{1,0:T(8,128)(2,1)} reshape(bf16[640,2,1760]{2,1,0:T(2,128)(2,1)} %all-to-all-done.3) | data formatting | bytes 9011200 | tf_op jit(solution)/shard_map/reshape | solution.py:147
  973.8 7.2 copy.112
  981.0 10.3 %reshape.249 = bf16[1280,1760]{1,0:T(8,128)(2,1)} reshape(bf16[640,2,1760]{2,1,0:T(2,128)(2,1)} %all-to-all-done.5) | data formatting | bytes 9011200 | tf_op jit(solution)/shard_map/reshape | solution.py:147
  991.3 7.2 copy.124
  998.5 9.0 fusion.32
  1007.5 6.3 fusion.30
  1013.8 6.7 maximum_bitcast_fusion
  (35 shorter events, 38.9 us)
Async XLA Ops:
  7.2 25.4 %copy-start = (bf16[384,384]{1,0:T(8,128)(2,1)S(1)}, bf16[384,384]{1,0:T(8,128)(2,1)}, u32[]{:S(2)}) copy-start(bf16[384,384]{1,0:T(8,128)(2,1)} %param.11) | copy-start | bytes 884740
  32.5 23.3 %copy-start.6 = (bf16[176,384]{1,0:T(8,128)(2,1)S(1)}, bf16[176,384]{1,0:T(8,128)(2,1)}, u32[]{:S(2)}) copy-start(bf16[176,384]{1,0:T(8,128)(2,1)} %param.12) | copy-start | bytes 405508
  83.7 38.6 %copy-start.4 = (bf16[176,384]{1,0:T(8,128)(2,1)S(1)}, bf16[176,384]{1,0:T(8,128)(2,1)}, u32[]{:S(2)}) copy-start(bf16[176,384]{1,0:T(8,128)(2,1)} %param.10) | copy-start | bytes 405508
  134.7 138.9 %all-to-all-start = ((bf16[4,88,6400]{2,1,0:T(8,128)(2,1)}), bf16[4,88,6400]{2,1,0:T(8,128)(2,1)}, u32[]{:S(2)}, u32[]{:S(2)}) async-start(bf16[4,88,6400]{2,1,0:T(8,128)(2,1)} %bitcast.153), calls=%async_computation | async-start | bytes 9011200 | tf_op jit(solution)/shard_map/all_to_all | solution.py:101
  141.5 12.2 %copy-start.5 = (s32[640]{0:T(1024)S(1)}, s32[640]{0:T(1024)}, u32[]{:S(2)}) copy-start(s32[640]{0:T(1024)} %param.15) | copy-start | bytes 7684
  273.7 105.4 %all-to-all-start.1 = ((bf16[4,88,6400]{2,1,0:T(8,128)(2,1)}), bf16[4,88,6400]{2,1,0:T(8,128)(2,1)}, u32[]{:S(2)}, u32[]{:S(2)}) async-start(bf16[4,88,6400]{2,1,0:T(8,128)(2,1)} %bitcast.154), calls=%async_computation.1 | async-start | bytes 9011200 | tf_op jit(solution)/shard_map/all_to_all | solution.py:101
  379.1 104.4 %all-to-all-start.2 = ((bf16[640,2,1760]{2,1,0:T(2,128)(2,1)}), bf16[640,2,1760]{2,1,0:T(2,128)(2,1)}, u32[]{:S(2)}, u32[]{:S(2)}) async-start(bf16[640,2,1760]{2,1,0:T(2,128)(2,1)} %reshape.234), calls=%async_computation.2 | async-start | bytes 9175040 | tf_op jit(solution)/shard_map/all_to_all | solution.py:127
  483.5 155.5 %all-to-all-start.4 = ((bf16[640,2,1760]{2,1,0:T(2,128)(2,1)}), bf16[640,2,1760]{2,1,0:T(2,128)(2,1)}, u32[]{:S(2)}, u32[]{:S(2)}) async-start(bf16[640,2,1760]{2,1,0:T(2,128)(2,1)} %reshape.243), calls=%async_computation.4 | async-start | bytes 9175040 | tf_op jit(solution)/shard_map/all_to_all | solution.py:127
  639.0 136.9 %all-to-all-start.3 = ((bf16[640,2,1760]{2,1,0:T(2,128)(2,1)}), bf16[640,2,1760]{2,1,0:T(2,128)(2,1)}, u32[]{:S(2)}, u32[]{:S(2)}) async-start(bf16[640,2,1760]{2,1,0:T(2,128)(2,1)} %reshape.255), calls=%async_computation.3 | async-start | bytes 9175040 | tf_op jit(solution)/shard_map/all_to_all | solution.py:142
  775.8 205.2 %all-to-all-start.5 = ((bf16[640,2,1760]{2,1,0:T(2,128)(2,1)}), bf16[640,2,1760]{2,1,0:T(2,128)(2,1)}, u32[]{:S(2)}, u32[]{:S(2)}) async-start(bf16[640,2,1760]{2,1,0:T(2,128)(2,1)} %reshape.256), calls=%async_computation.5 | async-start | bytes 9175040 | tf_op jit(solution)/shard_map/all_to_all | solution.py:142
  781.7 177.9 %all-reduce.3.cloned.1.call-start = ((), (), s32[]{:S(2)}) async-start(), calls=%async_computation.6 | async-start | bytes 2260992 | tf_op jit(solution)/shard_map/psum | solution.py:111
  998.5 9.0 copy-start.2
  998.5 9.0 copy-start.3
  1013.8 6.7 copy-start.1
Sparse Core Ops, SparseCore 0:
  788.9 170.6 all-reduce.2
where the time goes:
time: 1040 us; the launch traced here: 1030 us
  local copies, waits for them, and re-layouts  375 us (36%)
  matrix products  330 us (32%)
  waiting for transfers between devices  222 us (21%)
  other arithmetic  53.1 us (5%)
  starting transfers between devices  33.9 us (3%)
  between operations  14.6 us (1%)
    psum x1, waiting for transfers between devices, on_device(): totals = lax.psum(partials, both_axes)  177 us
    dot_general x3, matrix products, first_dims(): lax.dot_general(left, right, (((0,), (0,)), ((), ())), preferred_element_...  76.5 us
    dot_general x3, matrix products, last_dims(): lax.dot_general(left, right, (((1,), (1,)), ((), ())), preferred_element_...  56.3 us
    reshape x4, local copies, waits for them, and re-layouts, on_device(): rows = rows.reshape(waves, 2, sub * levels)  47.4 us
    dot_general x1, matrix products, on_device(): back_first = jnp.dot(weight_mid, delta_second, preferred_element_type=F32)  38.6 us
    dot_general x2, matrix products, on_device(): jnp.einsum('srql,sil->siqr', solved, table, preferred_element_type=F32)  29.8 us
    cos x2, other arithmetic, wave_tables(): return (jnp.cos(angles), jnp.sin(angles))  29.1 us
    convert_element_type x2, local copies, waits for them, and re-layouts, on_device(): jnp.einsum('srql,sil->siqr', solved, table, preferred_element_type=F32)  28.5 us
  transfers between devices with their start and end apart: 7, of which 3 were waited for; matrix products, arithmetic and copies ran while one was open for 57% of the time, Pallas kernels for 0%

commit v1 on v0

--- a/solution.py
+++ b/solution.py
@@ -129,6 +129,8 @@
 
     zonal = []
     for a in range(fields):
+        if a == fields - 1:
+            totals, gathered[a] = lax.optimization_barrier((totals, gathered[a]))
         fourier = gathered[a].reshape(n_dev, slot_count, 2, sub, levels)
         fourier = fourier.transpose(1, 2, 4, 0, 3).reshape(slot_count, 2 * levels, nlat)
         coeffs = jnp.einsum("sfi,sil->sfl", fourier, table, preferred_element_type=F32).astype(BF)

time: 1040 us -> 1120 us (1.077)
  waiting for transfers between devices: 222 us -> 303 us
    all_to_all x2, waiting for transfers between devices: 0.01 us -> 81.2 us  [on_device(): lax.all_to_all(rows, both_axes, split_axis=0, concat_axis=0, tiled=True)]
  transfers between devices with their start and end apart: 7 -> 7, of which waited for: 3 -> 4; matrix products, arithmetic and copies ran while one was open for 57% -> 53% of each run, Pallas kernels for 0% -> 0%
where the time goes in v1:
time: 1120 us; the launch traced here: 1110 us
  local copies, waits for them, and re-layouts  375 us (33%)
  matrix products  330 us (29%)
  waiting for transfers between devices  303 us (27%)
  other arithmetic  51 us (5%)
  starting transfers between devices  32.7 us (3%)
  between operations  14.6 us (1%)
    psum x1, waiting for transfers between devices, on_device(): totals = lax.psum(partials, both_axes)  177 us
    all_to_all x2, waiting for transfers between devices, on_device(): lax.all_to_all(rows, both_axes, split_axis=0, concat_axis=0, tiled=True)  81.2 us
    dot_general x3, matrix products, first_dims(): lax.dot_general(left, right, (((0,), (0,)), ((), ())), preferred_element_...  76.5 us
    dot_general x3, matrix products, last_dims(): lax.dot_general(left, right, (((1,), (1,)), ((), ())), preferred_element_...  56.3 us
    reshape x4, local copies, waits for them, and re-layouts, on_device(): rows = rows.reshape(waves, 2, sub * levels)  47.4 us
    dot_general x1, matrix products, on_device(): back_first = jnp.dot(weight_mid, delta_second, preferred_element_type=F32)  38.6 us
    dot_general x2, matrix products, on_device(): jnp.einsum('srql,sil->siqr', solved, table, preferred_element_type=F32)  30 us
    cos x2, other arithmetic, wave_tables(): return (jnp.cos(angles), jnp.sin(angles))  29.1 us
  transfers between devices with their start and end apart: 7, of which 4 were waited for; matrix products, arithmetic and copies ran while one was open for 53% of the time, Pallas kernels for 0%

profile of v1, /device:TPU:0, one launch (start us, length us, event | category | flops | bytes accessed | tf_op | source)
XLA Modules:
  0.0 1106.3 jit_solution(5246842083100895696)
XLA Ops:
  7.2 25.3 %multiply_convert_fusion = (bf16[384,25600]{1,0:T(8,128)(2,1)}, f32[384,25600]{1,0:T(8,128)}) fusion(bf16[176,384]{1,0:T(8,128)(2,1)} %param.10, bf16[176,25600]{1,0:T(8,128)(2,1)} %param.8), kind=kOutput, calls=%fused_computation.17 | convolution fusion | flops 3509452800 | bytes 68128768 | tf_op jit(solution)/shard_map/dot_general | solution.py:18
  32.5 23.3 %fusion.62 = f32[25600,384]{0,1:T(8,128)} fusion(bf16[384,25600]{1,0:T(8,128)(2,1)} %get-tuple-element.37, bf16[384,384]{1,0:T(8,128)(2,1)S(1)} %copy-done), kind=kOutput, calls=%fused_computation.91 | convolution fusion | flops 7549747200 | bytes 59277312 | tf_op jit(solution)/shard_map/dot_general | solution.py:18
  55.8 27.9 %fusion.7 = bf16[384,25600]{1,0:T(8,128)(2,1)} fusion(f32[25600,384]{0,1:T(8,128)} %fusion.62, bf16[176,384]{1,0:T(8,128)(2,1)S(1)} %copy-done.9, bf16[176,25600]{1,0:T(8,128)(2,1)} %param.9), kind=kOutput, calls=%fused_computation.15 | convolution fusion | flops 3548774400 | bytes 68128768 | tf_op jit(solution)/shard_map/dot_general | solution.py:18
  83.6 38.6 %fusion = bf16[384,25600]{1,0:T(8,128)(2,1)} fusion(f32[384,25600]{1,0:T(8,128)} %get-tuple-element.38, bf16[384,384]{1,0:T(8,128)(2,1)S(1)} %copy-done, bf16[384,25600]{1,0:T(8,128)(2,1)} %fusion.7), kind=kOutput, calls=%fused_computation.5 | convolution fusion | flops 7638220800 | bytes 78938112 | tf_op jit(solution)/shard_map/dot_general | solution.py:78
  122.3 10.0 convolution_convert_fusion.1
  134.7 6.8 all-to-all-start
  141.5 12.2 %convolution_convert_fusion = bf16[25600,88]{0,1:T(8,128)(2,1)} fusion(bf16[384,25600]{1,0:T(8,128)(2,1)} %fusion, bf16[176,384]{1,0:T(8,128)(2,1)S(1)} %copy-done.7), kind=kOutput, calls=%fused_computation.28 | convolution fusion | flops 1732403200 | bytes 24233984 | tf_op jit(solution)/shard_map/dot_general | solution.py:97
  153.7 13.3 %fusion.39 = (f32[1280,640,1]{1,0,2:T(8,128)S(1)}, f32[1280,640,1]{1,0,2:T(8,128)S(1)}) fusion(s32[640]{0:T(1024)S(1)} %copy-done.8), kind=kLoop, calls=%fused_computation.69 | loop fusion | flops 8192000 | bytes 6556160 | tf_op jit(solution)/shard_map/cos | solution.py:30
  167.0 15.8 %fusion.36 = (f32[640,1,1280]{2,0,1:T(8,128)}, f32[640,1,1280]{2,0,1:T(8,128)}) fusion(s32[640]{0:T(1024)S(1)} %copy-done.8), kind=kLoop, calls=%fused_computation.64 | loop fusion | flops 8192000 | bytes 6556160 | tf_op jit(solution)/shard_map/cos | solution.py:30
  185.2 10.5 copy.95
  195.7 7.8 convert_element_type.106
  208.3 6.1 pad_maximum_fusion
  214.5 10.6 copy.99
  225.0 8.8 stack.14
  239.2 16.2 %convolution_bitcast_fusion = f32[176,384]{1,0:T(8,128)} fusion(bf16[384,25600]{1,0:T(8,128)(2,1)} %fusion, bf16[176,25600]{1,0:T(8,128)(2,1)} %param.8), kind=kOutput, calls=%fused_computation.77 | convolution fusion | flops 3460300800 | bytes 28942336 | tf_op jit(solution)/shard_map/dot_general | solution.py:22
  255.4 18.2 %fusion.63 = f32[384,384]{1,0:T(8,128)} fusion(bf16[384,25600]{1,0:T(8,128)(2,1)} %get-tuple-element.37, bf16[384,25600]{1,0:T(8,128)(2,1)} %fusion.7), kind=kOutput, calls=%fused_computation.92 | convolution fusion | flops 7549747200 | bytes 39911424 | tf_op jit(solution)/shard_map/dot_general | solution.py:22
  279.2 21.8 %fusion.50 = f32[176,384]{1,0:T(8,128)} fusion(bf16[176,25600]{1,0:T(8,128)(2,1)} %param.9, f32[25600,384]{0,1:T(8,128)} %fusion.62), kind=kOutput, calls=%fused_computation.76 | convolution fusion | flops 3509452800 | bytes 48603136 | tf_op jit(solution)/shard_map/dot_general | solution.py:22
  301.0 10.7 reshape.235
  311.7 9.4 copy.103
  321.1 9.8 reshape.236
  330.8 10.2 convolution_convert_fusion.2
  341.1 7.4 copy.104
  348.5 10.0 reshape.237
  358.5 20.7 %all-to-all-done.1 = bf16[4,88,6400]{2,1,0:T(8,128)(2,1)} async-done(((bf16[4,88,6400]{2,1,0:T(8,128)(2,1)}), bf16[4,88,6400]{2,1,0:T(8,128)(2,1)}, u32[]{:S(2)}, u32[]{:S(2)}) %all-to-all-start.1) | async-done | bytes 4505632 | tf_op jit(solution)/shard_map/all_to_all | solution.py:101
  383.0 19.7 %fusion.12 = bf16[20,640,640]{2,1,0:T(8,128)(2,1)} fusion(s32[20]{0:T(128)S(1)} %dynamic_slice.3, pred[640]{0:T(1024)(128)(4,1)S(1)} %iota_compare_fusion.3, bf16[20,320,640]{2,1,0:T(8,128)(2,1)} %param.13), kind=kOutput, calls=%fused_computation.22 | convolution fusion | flops 5399347200 | bytes 24576720 | tf_op jit(solution)/shard_map/pi,sil->spl/dot_general | solution.py:38
  402.7 10.7 reshape.232
  413.4 9.4 copy.101
  422.8 9.8 reshape.233
  432.6 10.3 convolution_convert_fusion.3
  442.9 7.2 copy.102
  450.1 10.2 reshape.234
  460.3 23.2 %all-to-all-done.3 = bf16[640,2,1760]{2,1,0:T(2,128)(2,1)} async-done(((bf16[640,2,1760]{2,1,0:T(2,128)(2,1)}), bf16[640,2,1760]{2,1,0:T(2,128)(2,1)}, u32[]{:S(2)}, u32[]{:S(2)}) %all-to-all-start.3) | async-done | bytes 4505632 | tf_op jit(solution)/shard_map/all_to_all | solution.py:127
  483.5 6.0 all-to-all-start.2
  489.4 18.8 %copy.128 = bf16[640,88,88,1]{2,1,3,0:T(8,128)(2,1)} copy(bf16[640,88,88,1]{0,2,1,3:T(8,128)(2,1)} %bitcast.155) | data formatting | bytes 19824640 | tf_op jit(solution)/shard_map/optimization_barrier | solution.py:117
  513.2 13.0 %reshape.238 = bf16[32,20,2,20,88]{4,3,1,0,2:T(8,128)(2,1)} reshape(bf16[640,2,1760]{2,0,1:T(8,128)(2,1)} %copy.105) | data formatting | bytes 9011200 | tf_op jit(solution)/shard_map/reshape | solution.py:134
  526.2 11.0 copy.106
  537.2 13.6 %reshape.239 = bf16[20,176,640]{1,2,0:T(8,128)(2,1)} reshape(bf16[20,2,88,32,20]{2,1,4,3,0:T(2,128)(2,1)} %copy.106) | data formatting | bytes 9011200 | tf_op jit(solution)/shard_map/reshape | solution.py:135
  550.8 13.9 %convolution_convert_fusion.5 = bf16[20,176,640]{2,1,0:T(8,128)(2,1)} fusion(bf16[20,176,640]{1,2,0:T(8,128)(2,1)} %reshape.239, bf16[20,640,640]{2,1,0:T(8,128)(2,1)} %fusion.12), kind=kOutput, calls=%fused_computation.73 | convolution fusion | flops 2885836800 | bytes 25395200 | tf_op jit(solution)/shard_map/sfi,sil->sfl/dot_general | solution.py:136
  564.7 10.0 copy.109
  574.7 11.6 %convert_bitcast_fusion.1 = bf16[20,2,88,640]{2,0,1,3:T(8,128)(2,1)} fusion(bf16[640,88,88,1]{2,1,3,0:T(8,128)(2,1)} %copy.128, bf16[20,2,88,640]{2,0,1,3:T(8,128)(2,1)} %copy.109), kind=kOutput, calls=%fused_computation.37 | convolution fusion | flops 398745600 | bytes 18923520 | tf_op jit(solution)/shard_map/srkl,lkq->srql/dot_general | solution.py:138
  586.4 15.1 %convert_bitcast_fusion.3 = bf16[20,640,88,2]{1,2,3,0:T(8,128)(2,1)} fusion(bf16[20,2,88,640]{2,0,1,3:T(8,128)(2,1)} %convert_bitcast_fusion.1, bf16[20,640,640]{2,1,0:T(8,128)(2,1)} %fusion.12), kind=kOutput, calls=%fused_computation.51 | convolution fusion | flops 2885836800 | bytes 25395200 | tf_op jit(solution)/shard_map/srql,sil->siqr/dot_general | solution.py:141
  601.5 14.2 %copy.111 = bf16[20,640,88,2]{2,3,1,0:T(2,128)(2,1)} copy(bf16[20,640,88,2]{1,2,3,0:T(8,128)(2,1)} %convert_bitcast_fusion.3) | data formatting | bytes 9011200 | tf_op jit(solution)/shard_map/convert_element_type | solution.py:141
  615.8 7.9 copy.134
  623.7 15.7 %reshape.255 = bf16[640,2,1760]{2,1,0:T(2,128)(2,1)} reshape(bf16[32,20,2,20,88]{4,3,2,1,0:T(8,128)(2,1)} %copy.134) | data formatting | bytes 9011200 | tf_op jit(solution)/shard_map/reshape | solution.py:143
  639.4 5.9 all-to-all-start.4
  646.0 177.2 %all-reduce.3.cloned.1.call-done = (f32[176,384]{1,0:T(8,128)}, f32[384,384]{1,0:T(8,128)}, f32[176,384]{1,0:T(8,128)}) async-done(((f32[176,384]{1,0:T(8,128)}, f32[384,384]{1,0:T(8,128)}, f32[176,384]{1,0:T(8,128)}), (f32[176,384]{1,0:T(8,128)}, f32[384,384]{1,0:T(8,128)}, f32[176,384]{1,0:T(8,128)})) %all-reduce.3.cloned.1.call-update) | async-done | bytes 1130512 | tf_op jit(solution)/shard_map/psum | solution.py:111
  828.2 13.1 %reshape.244 = bf16[32,20,2,20,88]{4,3,1,0,2:T(8,128)(2,1)} reshape(bf16[640,2,1760]{2,0,1:T(8,128)(2,1)} %copy.115) | data formatting | bytes 9011200 | tf_op jit(solution)/shard_map/reshape | solution.py:134
  841.3 11.0 copy.116
  852.3 13.6 %reshape.245 = bf16[20,176,640]{1,2,0:T(8,128)(2,1)} reshape(bf16[20,2,88,32,20]{2,1,4,3,0:T(2,128)(2,1)} %copy.116) | data formatting | bytes 9011200 | tf_op jit(solution)/shard_map/reshape | solution.py:135
  866.0 13.9 %convolution_convert_fusion.4 = bf16[20,176,640]{2,1,0:T(8,128)(2,1)} fusion(bf16[20,176,640]{1,2,0:T(8,128)(2,1)} %reshape.245, bf16[20,640,640]{2,1,0:T(8,128)(2,1)} %fusion.12), kind=kOutput, calls=%fused_computation.72 | convolution fusion | flops 2885836800 | bytes 25395200 | tf_op jit(solution)/shard_map/sfi,sil->sfl/dot_general | solution.py:136
  879.9 10.0 copy.119
  889.9 11.6 %convert_bitcast_fusion = bf16[20,2,88,640]{2,0,1,3:T(8,128)(2,1)} fusion(bf16[640,88,88,1]{2,1,3,0:T(8,128)(2,1)} %copy.128, bf16[20,2,88,640]{2,0,1,3:T(8,128)(2,1)} %copy.119), kind=kOutput, calls=%fused_computation.36 | convolution fusion | flops 398745600 | bytes 18923520 | tf_op jit(solution)/shard_map/srkl,lkq->srql/dot_general | solution.py:138
  901.5 14.9 %convert_bitcast_fusion.2 = bf16[20,640,88,2]{1,2,3,0:T(8,128)(2,1)} fusion(bf16[20,2,88,640]{2,0,1,3:T(8,128)(2,1)} %convert_bitcast_fusion, bf16[20,640,640]{2,1,0:T(8,128)(2,1)} %fusion.12), kind=kOutput, calls=%fused_computation.50 | convolution fusion | flops 2885836800 | bytes 25395200 | tf_op jit(solution)/shard_map/srql,sil->siqr/dot_general | solution.py:141
  916.4 14.2 %copy.121 = bf16[20,640,88,2]{2,3,1,0:T(2,128)(2,1)} copy(bf16[20,640,88,2]{1,2,3,0:T(8,128)(2,1)} %convert_bitcast_fusion.2) | data formatting | bytes 9011200 | tf_op jit(solution)/shard_map/convert_element_type | solution.py:141
  930.7 8.1 copy.137
  938.7 15.8 %reshape.256 = bf16[640,2,1760]{2,1,0:T(2,128)(2,1)} reshape(bf16[32,20,2,20,88]{4,3,2,1,0:T(8,128)(2,1)} %copy.137) | data formatting | bytes 9011200 | tf_op jit(solution)/shard_map/reshape | solution.py:143
  960.9 10.3 reshape.243
  971.2 7.2 copy.114
  978.4 81.2 %all-to-all-done.5 = bf16[640,2,1760]{2,1,0:T(2,128)(2,1)} async-done(((bf16[640,2,1760]{2,1,0:T(2,128)(2,1)}), bf16[640,2,1760]{2,1,0:T(2,128)(2,1)}, u32[]{:S(2)}, u32[]{:S(2)}) %all-to-all-start.5) | async-done | bytes 4505632 | tf_op jit(solution)/shard_map/all_to_all | solution.py:144
  1059.6 10.3 reshape.249
  1069.9 7.2 copy.124
  1077.1 9.0 fusion.32
  1086.1 6.3 fusion.30
  1092.4 6.7 maximum_bitcast_fusion
  (41 shorter events, 41.4 us)
Async XLA Ops:
  7.2 25.4 %copy-start = (bf16[384,384]{1,0:T(8,128)(2,1)S(1)}, bf16[384,384]{1,0:T(8,128)(2,1)}, u32[]{:S(2)}) copy-start(bf16[384,384]{1,0:T(8,128)(2,1)} %param.11) | copy-start | bytes 884740
  32.5 23.3 %copy-start.9 = (bf16[176,384]{1,0:T(8,128)(2,1)S(1)}, bf16[176,384]{1,0:T(8,128)(2,1)}, u32[]{:S(2)}) copy-start(bf16[176,384]{1,0:T(8,128)(2,1)} %param.12) | copy-start | bytes 405508
  83.6 38.7 %copy-start.7 = (bf16[176,384]{1,0:T(8,128)(2,1)S(1)}, bf16[176,384]{1,0:T(8,128)(2,1)}, u32[]{:S(2)}) copy-start(bf16[176,384]{1,0:T(8,128)(2,1)} %param.10) | copy-start | bytes 405508
  134.7 139.0 %all-to-all-start = ((bf16[4,88,6400]{2,1,0:T(8,128)(2,1)}), bf16[4,88,6400]{2,1,0:T(8,128)(2,1)}, u32[]{:S(2)}, u32[]{:S(2)}) async-start(bf16[4,88,6400]{2,1,0:T(8,128)(2,1)} %bitcast.153), calls=%async_computation | async-start | bytes 9011200 | tf_op jit(solution)/shard_map/all_to_all | solution.py:101
  141.5 12.2 %copy-start.8 = (s32[640]{0:T(1024)S(1)}, s32[640]{0:T(1024)}, u32[]{:S(2)}) copy-start(s32[640]{0:T(1024)} %param.15) | copy-start | bytes 7684
  273.7 105.4 %all-to-all-start.1 = ((bf16[4,88,6400]{2,1,0:T(8,128)(2,1)}), bf16[4,88,6400]{2,1,0:T(8,128)(2,1)}, u32[]{:S(2)}, u32[]{:S(2)}) async-start(bf16[4,88,6400]{2,1,0:T(8,128)(2,1)} %bitcast.154), calls=%async_computation.1 | async-start | bytes 9011200 | tf_op jit(solution)/shard_map/all_to_all | solution.py:101
  379.1 104.4 %all-to-all-start.3 = ((bf16[640,2,1760]{2,1,0:T(2,128)(2,1)}), bf16[640,2,1760]{2,1,0:T(2,128)(2,1)}, u32[]{:S(2)}, u32[]{:S(2)}) async-start(bf16[640,2,1760]{2,1,0:T(2,128)(2,1)} %reshape.237), calls=%async_computation.3 | async-start | bytes 9175040 | tf_op jit(solution)/shard_map/all_to_all | solution.py:127
  483.5 155.9 %all-to-all-start.2 = ((bf16[640,2,1760]{2,1,0:T(2,128)(2,1)}), bf16[640,2,1760]{2,1,0:T(2,128)(2,1)}, u32[]{:S(2)}, u32[]{:S(2)}) async-start(bf16[640,2,1760]{2,1,0:T(2,128)(2,1)} %reshape.234), calls=%async_computation.2 | async-start | bytes 9175040 | tf_op jit(solution)/shard_map/all_to_all | solution.py:127
  639.4 315.1 %all-to-all-start.4 = ((bf16[640,2,1760]{2,1,0:T(2,128)(2,1)}), bf16[640,2,1760]{2,1,0:T(2,128)(2,1)}, u32[]{:S(2)}, u32[]{:S(2)}) async-start(bf16[640,2,1760]{2,1,0:T(2,128)(2,1)} %reshape.255), calls=%async_computation.4 | async-start | bytes 9175040 | tf_op jit(solution)/shard_map/all_to_all | solution.py:144
  645.3 177.9 %all-reduce.3.cloned.1.call-start = ((), (), s32[]{:S(2)}) async-start(), calls=%async_computation.6 | async-start | bytes 2260992 | tf_op jit(solution)/shard_map/psum | solution.py:111
  938.7 20.4 %copy-start.5 = (f32[176,384]{1,0:T(8,128)S(1)}, f32[176,384]{1,0:T(8,128)}, u32[]{:S(2)}) copy-start(f32[176,384]{1,0:T(8,128)} %get-tuple-element.22) | copy-start | bytes 811012
  938.7 20.4 %copy-start.6 = (f32[176,384]{1,0:T(8,128)S(1)}, f32[176,384]{1,0:T(8,128)}, u32[]{:S(2)}) copy-start(f32[176,384]{1,0:T(8,128)} %get-tuple-element.24) | copy-start | bytes 811012
  954.5 5.5 copy-start.4
  954.5 105.1 %all-to-all-start.5 = ((bf16[640,2,1760]{2,1,0:T(2,128)(2,1)}), bf16[640,2,1760]{2,1,0:T(2,128)(2,1)}, u32[]{:S(2)}, u32[]{:S(2)}) async-start(bf16[640,2,1760]{2,1,0:T(2,128)(2,1)} %reshape.256), calls=%async_computation.5 | async-start | bytes 9175040 | tf_op jit(solution)/shard_map/all_to_all | solution.py:144
  1077.1 9.0 copy-start.2
  1077.1 9.0 copy-start.3
  1092.4 6.7 copy-start.1
Sparse Core Ops, SparseCore 0:
  652.5 170.6 all-reduce.2
